TPU v7x, 128 devices: a whole 4x4x4 slice. The times are simulated.
128 devices in a mesh: dp: 32 (over z, x, core), head: 4 (over y).
Axes of the slice: x: 4, y: 4, z: 4, core: 2. Of those that a mesh axis runs over, the one named last changes fastest.
Arguments:
- hidden: bfloat16 [1024, 2048], P('dp'), may hold values from -6 to 6
- attn_gain: float32 [2048], replicated, may hold values from 0.1 to 1.9
- w_query: bfloat16 [2048, 3072], P(None, 'head'), may hold values from -0.125 to 0.125
- w_latent: bfloat16 [2048, 576], P(None, 'head'), may hold values from -0.125 to 0.125
- latent_gain: float32 [512], replicated, may hold values from 0.1 to 1.9
- w_key_up: bfloat16 [16, 128, 512], P('head'), may hold values from -0.5 to 0.5
- w_value_up: bfloat16 [16, 512, 128], P('head'), may hold values from -0.25 to 0.25
- w_out: bfloat16 [2048, 2048], P('head'), may hold values from -0.125 to 0.125
- kv_cache: bfloat16 [1024, 128, 576], P('dp'), may hold values from -110 to 110
- lengths: int32 [1024], P('dp'), may hold values from 1 to 128, 65536 in all
- live_mask: int32 [1024], P('dp'), may hold values 0 or 1
- mlp_gain: float32 [2048], replicated, may hold values from 0.1 to 1.9
- w_router: bfloat16 [2048, 64], replicated, may hold values from -0.125 to 0.125
- routes: int32 [1024, 6], P('dp'), may hold values from 0 to 63, all different within a row; in each aligned block of 32 rows (0 to 31, 32 to 63, ...) at most 6 rows name the same one
- w_experts_in: bfloat16 [64, 2048, 2, 1408], P('dp', None, None, 'head'), may hold values from -0.125 to 0.125
- w_experts_out: bfloat16 [64, 1408, 2048], P('dp', 'head'), may hold values from -0.15625 to 0.15625
- w_shared_in: bfloat16 [2048, 2, 1408], P(None, None, 'head'), may hold values from -0.125 to 0.125
- w_shared_out: bfloat16 [1408, 2048], P('head'), may hold values from -0.15625 to 0.15625
Outputs:
- output: bfloat16 [1024, 2048], P('dp', 'head')
Inputs may be any that keep to these rules, and one draw needn't show every extreme that they name: Among the routes of one device's 32 rows no expert is named more than 6 times, a bound that some block reaches. Request t has cached positions 0 to lengths[t] - 1; some request has 128.
All inputs are finite; a program needn't handle non-finite values. No bound on the sum of `lengths` or of `live_mask` on one device may be relied on, other than what follows from the above.
Results may differ from a plain program's by a relative error of at most 0.02.
The roundings to bfloat16 on the way count: a program that leaves them out, or rounds other values in their place, can miss the bound.
Values may be sent and summed in bfloat16 or wider, within the bound.
A program may use at most 128 MiB of HBM per device.

v0:
```python
import math
import jax
import jax.numpy as jnp
from jax import lax
from jax.sharding import PartitionSpec as P

NOPE = 128
ROPE = 64
VDIM = 128
LAT = 512
norm_eps = 1e-06
rope_theta = 50000.0
route_scale = 2.446


def rms_norm(values, weights):
    mean_square = jnp.mean(values * values, axis=-1, keepdims=True)
    return values * lax.rsqrt(mean_square + norm_eps) * weights


def rotary(values, positions):
    half_size = values.shape[-1] // 2
    frequency = rope_theta ** (-jnp.arange(half_size, dtype=jnp.float32) / half_size)
    angles = positions.reshape((-1,) + (1,) * (values.ndim - 1)) * frequency
    first_half = values[..., :half_size]
    second_half = values[..., half_size:]
    cosine = jnp.cos(angles)
    sine_part = jnp.sin(angles)
    return jnp.concatenate(
        [
            first_half * cosine - second_half * sine_part,
            second_half * cosine + first_half * sine_part,
        ],
        axis=-1,
    )


def body(
    hidden,
    attn_gain,
    w_query,
    w_latent,
    latent_gain,
    w_key_up,
    w_value_up,
    w_out,
    kv_cache,
    lengths,
    live_mask,
    mlp_gain,
    w_router,
    routes,
    w_experts_in,
    w_experts_out,
    w_shared_in,
    w_shared_out,
):
    request_count = hidden.shape[0]
    model_width = hidden.shape[1]
    local_heads = w_key_up.shape[0]
    cache_length = kv_cache.shape[1]
    head_count = lax.axis_size("head")
    share_width = model_width // head_count
    column_start = lax.axis_index("head") * share_width
    dp_count = lax.axis_size("dp")
    local_experts = w_experts_in.shape[0]
    expert_total = local_experts * dp_count
    top_count = routes.shape[1]
    capacity = max(2, 2 * top_count * request_count // expert_total)
    normed = rms_norm(hidden.astype(jnp.float32), attn_gain).astype(jnp.bfloat16)
    query_all = jnp.dot(normed, w_query, preferred_element_type=jnp.float32).reshape(
        request_count, local_heads, NOPE + ROPE
    )
    positions = lengths.astype(jnp.float32)
    query_nope = query_all[..., :NOPE].astype(jnp.bfloat16)
    query_rope = rotary(query_all[..., NOPE:], positions).astype(jnp.bfloat16)
    query_latent = jnp.einsum(
        "rhn,hnc->rhc", query_nope, w_key_up, preferred_element_type=jnp.float32
    ).astype(jnp.bfloat16)
    fresh_part = jnp.dot(normed, w_latent, preferred_element_type=jnp.float32).astype(jnp.bfloat16)
    fresh_kv = lax.all_gather(fresh_part, "head", axis=1, tiled=True)
    latent_new = rms_norm(fresh_kv[:, :LAT].astype(jnp.float32), latent_gain)
    rope_new = rotary(fresh_kv[:, LAT:].astype(jnp.float32), positions)
    key_new = jnp.concatenate([latent_new, rope_new], axis=-1).astype(jnp.bfloat16)
    query_full = jnp.concatenate([query_latent, query_rope], axis=-1)
    inverse_root = 1.0 / math.sqrt(NOPE + ROPE)
    scores = (
        jnp.einsum("rhc,rjc->rhj", query_full, kv_cache, preferred_element_type=jnp.float32)
        * inverse_root
    )
    in_cache = jnp.arange(cache_length, dtype=jnp.int32)[None, :] < lengths[:, None]
    scores = jnp.where(in_cache[:, None, :], scores, -jnp.inf)
    score_new = (
        jnp.einsum("rhc,rc->rh", query_full, key_new, preferred_element_type=jnp.float32)
        * inverse_root
    )
    highest = jnp.maximum(jnp.max(scores, axis=-1), score_new)
    weights_cached = jnp.exp(scores - highest[..., None])
    weight_new = jnp.exp(score_new - highest)
    denominator = jnp.sum(weights_cached, axis=-1) + weight_new
    probabilities = (weights_cached / denominator[..., None]).astype(jnp.bfloat16)
    prob_new = (weight_new / denominator).astype(jnp.bfloat16)
    context = jnp.einsum(
        "rhj,rjc->rhc", probabilities, kv_cache[..., :LAT], preferred_element_type=jnp.float32
    )
    context = (
        context
        + prob_new.astype(jnp.float32)[..., None] * key_new[:, None, :LAT].astype(jnp.float32)
    ).astype(jnp.bfloat16)
    values = jnp.einsum(
        "rhc,hcv->rhv", context, w_value_up, preferred_element_type=jnp.float32
    ).astype(jnp.bfloat16)
    partial_value = jnp.dot(
        values.reshape(request_count, local_heads * VDIM), w_out, preferred_element_type=jnp.float32
    )
    attention = lax.psum(partial_value.astype(jnp.bfloat16), "head").astype(jnp.float32)
    mixed_rows = (hidden.astype(jnp.float32) + attention).astype(jnp.bfloat16)
    ffn_input = rms_norm(mixed_rows.astype(jnp.float32), mlp_gain).astype(jnp.bfloat16)
    mixed_share = lax.dynamic_slice_in_dim(mixed_rows, column_start, share_width, 1)
    logits = jnp.dot(ffn_input, w_router, preferred_element_type=jnp.float32)
    chosen = jax.nn.sigmoid(jnp.take_along_axis(logits, routes, axis=1))
    route_weight = (
        route_scale
        * live_mask.astype(jnp.float32)[:, None]
        * chosen
        / jnp.sum(chosen, axis=1, keepdims=True)
    )
    pair_count = request_count * top_count
    flat_routes = routes.reshape(pair_count)
    live_pairs = jnp.repeat(live_mask, top_count)
    member = (
        (flat_routes[:, None] == jnp.arange(expert_total, dtype=jnp.int32)[None, :])
        & (live_pairs[:, None] == 1)
    ).astype(jnp.int32)
    earlier = jnp.cumsum(member, axis=0) - member
    slot_rank = jnp.sum(earlier * member, axis=1)
    slot_total = expert_total * capacity
    buffer_slot = jnp.where(live_pairs == 1, flat_routes * capacity + slot_rank, slot_total)
    token_of_pair = jnp.arange(pair_count, dtype=jnp.int32) // top_count
    spread = ffn_input[token_of_pair]
    packed = (
        jnp.zeros((slot_total, ffn_input.shape[1]), jnp.bfloat16)
        .at[buffer_slot]
        .set(spread, mode="drop")
    )
    arrived = lax.all_to_all(
        packed.reshape(dp_count, local_experts, capacity, ffn_input.shape[1]),
        "dp",
        split_axis=0,
        concat_axis=0,
        tiled=True,
    )
    gate_up = jnp.einsum(
        "secd,edkf->seckf", arrived, w_experts_in, preferred_element_type=jnp.float32
    )
    acting = (jax.nn.silu(gate_up[..., 0, :]) * gate_up[..., 1, :]).astype(jnp.bfloat16)
    expert_part = jnp.einsum(
        "secf,efd->secd", acting, w_experts_out, preferred_element_type=jnp.float32
    )
    expert_share = lax.psum_scatter(
        expert_part.astype(jnp.bfloat16), "head", scatter_dimension=3, tiled=True
    )
    returned = lax.all_to_all(expert_share, "dp", split_axis=0, concat_axis=0, tiled=True)
    returned_rows = returned.reshape(slot_total, share_width)
    pick_slot = jnp.minimum(buffer_slot, slot_total - 1)
    pair_rows = returned_rows[pick_slot].astype(jnp.float32)
    routed = jnp.sum(
        (route_weight.reshape(pair_count)[:, None] * pair_rows).reshape(
            request_count, top_count, share_width
        ),
        axis=1,
    )
    shared_width = w_shared_out.shape[0]
    shared_pair = jnp.dot(
        ffn_input,
        w_shared_in.reshape(model_width, 2 * shared_width),
        preferred_element_type=jnp.float32,
    ).reshape(request_count, 2, shared_width)
    shared_act = (jax.nn.silu(shared_pair[:, 0]) * shared_pair[:, 1]).astype(jnp.bfloat16)
    shared_part = jnp.dot(shared_act, w_shared_out, preferred_element_type=jnp.float32)
    shared_share = lax.psum_scatter(
        shared_part.astype(jnp.bfloat16), "head", scatter_dimension=1, tiled=True
    ).astype(jnp.float32)
    return (mixed_share.astype(jnp.float32) + shared_share + routed).astype(jnp.bfloat16)


def solution(mesh):
    placed = (
        P("dp", None),
        P(),
        P(None, "head"),
        P(None, "head"),
        P(),
        P("head", None, None),
        P("head", None, None),
        P("head", None),
        P("dp", None, None),
        P("dp"),
        P("dp"),
        P(),
        P(),
        P("dp", None),
        P("dp", None, None, "head"),
        P("dp", "head", None),
        P(None, None, "head"),
        P("head", None),
    )
    return jax.shard_map(
        body, mesh=mesh, in_specs=placed, out_specs=P("dp", "head"), check_vma=False
    )
```

profile of v0, /device:TPU:1, one launch (start us, length us, event | category | flops | bytes accessed | tf_op | source)
XLA Modules:
  0.0 187.7 jit_solution(8351223471823655975)
XLA Ops:
  6.6 0.8 convert_element_type.107
  7.4 0.9 iota_compare_fusion.2
  8.2 1.0 fusion.40
  9.3 1.5 fusion.29
  10.8 10.4 %all-gather = bf16[4,144,32]{1,2,0:T(8,128)(2,1)S(1)} all-gather(bf16[1,144,32]{1,2,0:T(8,128)(2,1)S(1)} %fusion.29), channel_id=1, replica_groups=mesh['dp'=32,'head'=4] {'head'}, dimensions={0}, use_global_device_ids=true | all-gather | bytes 46080 | tf_op jit(solution)/shard_map/all_gather | solution.py:81
  21.2 0.1 reshape.357
  21.3 0.1 fusion.50
  21.5 1.6 fusion.61
  23.0 0.1 reshape.311
  23.2 0.1 fusion.77
  23.3 0.1 fusion.75
  23.4 1.2 fusion.26
  24.7 0.1 subtract_convert_fusion.1
  24.8 0.1 maximum_bitcast_fusion
  24.9 0.1 pad_maximum_fusion
  25.0 0.3 fusion.46
  25.3 3.4 %fusion.78 = (f32[32,4]{1,0:T(8,128)S(1)}, f32[32,4,128]{2,1,0:T(4,128)S(1)}) fusion(bf16[32,128,576]{1,2,0:T(8,128)(2,1)} %param.26, bf16[32,4,576]{2,0,1:T(8,128)(2,1)S(1)} %pad_maximum_fusion, pred[32,128]{1,0:T(8,128)(4,1)S(1)} %iota_compare_fusion.2), kind=kOutput, calls=%fused_computation.128 | convolution fusion | flops 18923392 | bytes 4936192 | tf_op jit(solution)/shard_map/rhc,rjc->rhj/dot_general | solution.py:88
  28.7 0.2 fusion.57
  28.9 0.1 copy-done.1
  29.1 1.2 fusion.23
  30.3 0.2 fusion.28
  30.6 0.3 copy-done.3
  30.8 1.1 convolution_convert_fusion.1
  32.1 0.1 broadcast_in_dim.27
  32.1 0.1 eq.62
  32.2 0.1 eq.57
  32.4 0.1 copy.93
  32.5 0.1 copy.92
  32.6 0.1 mul.265
  32.7 0.1 eq.58
  32.8 0.6 reduce-window.6
  33.4 0.2 slice_reduce_fusion
  33.7 0.1 bitcast_bitcast_fusion
  33.8 41.9 %all-reduce.3.cloned.1.call-done = bf16[32,2048]{1,0:T(8,128)(2,1)} async-done(((bf16[32,2048]{1,0:T(8,128)(2,1)}), bf16[32,2048]{1,0:T(8,128)(2,1)}) %all-reduce.3.cloned.1.call-update) | async-done | bytes 131088 | tf_op jit(solution)/shard_map/psum | solution.py:116
  75.7 1.1 fusion.37
  76.8 0.6 copy-done.5
  77.4 0.1 fusion.39
  77.5 5.6 %scatter_custom_fusion = bf16[384,2048]{1,0:T(8,128)(2,1)} fusion(s32[192]{0:T(256)S(1)} %bitcast.114, bf16[32,2048]{1,0:T(8,128)(2,1)S(1)} %fusion.39, s32[1024]{0:T(1024)S(1)} %pad_clamp_fusion.1, bf16[]{:T(256)} %constant.75.clone.1), kind=kCustom, calls=%fused_computation.28 | custom fusion | bytes 1572866 | tf_op jit(solution)/shard_map/scatter | solution.py:144
  83.1 3.7 %reshape.317 = bf16[32,2,6,2048]{3,2,1,0:T(8,128)(2,1)} reshape(bf16[384,2048]{1,0:T(8,128)(2,1)} %scatter_custom_fusion) | data formatting | bytes 3145728 | tf_op jit(solution)/shard_map/reshape | solution.py:147
  86.8 3.2 %copy.96 = bf16[32,2,6,2048]{3,1,2,0:T(2,128)(2,1)S(1)} copy(bf16[32,2,6,2048]{3,2,1,0:T(8,128)(2,1)} %reshape.317) | data formatting | bytes 3145728 | tf_op jit(solution)/shard_map/reshape | solution.py:147
  90.0 32.3 %all_to_all.10 = bf16[32,2,6,2048]{3,1,2,0:T(2,128)(2,1)S(1)} all-to-all(bf16[32,2,6,2048]{3,1,2,0:T(2,128)(2,1)S(1)} %copy.96), channel_id=1, replica_groups=mesh['dp'=32,'head'=4] {'dp'}, dimensions={0} | all-to-all | bytes 3145728 | tf_op jit(solution)/shard_map/all_to_all | solution.py:146
  122.4 5.9 %fusion.15 = f32[32,2,6,2,352]{4,0,3,2,1:T(8,128)S(1)} fusion(bf16[2,2048,2,352]{1,3,2,0:T(8,128)(2,1)} %param.32, bf16[32,2,6,2048,1]{3,1,2,0,4:T(2,128)(2,1)S(1)} %bitcast.106), kind=kOutput, calls=%fused_computation.17 | convolution fusion | flops 1107296256 | bytes 8421376 | tf_op jit(solution)/shard_map/secd,edkf->seckf/dot_general | solution.py:153
  128.3 2.2 %fusion.11 = bf16[32,2,6,2048]{3,0,2,1:T(8,128)(2,1)} fusion(bf16[2,352,2048]{2,1,0:T(8,128)(2,1)S(1)} %copy-done.10, f32[32,2,6,2,352]{4,0,3,2,1:T(8,128)S(1)} %fusion.15), kind=kOutput, calls=%fused_computation.13 | convolution fusion | flops 555245568 | bytes 5537792 | tf_op jit(solution)/shard_map/secf,efd->secd/dot_general | solution.py:157
  130.5 0.1 copy.89
  130.6 0.1 reshape.337
  130.7 0.6 pad_clamp_fusion
  131.3 1.1 fusion.79
  132.4 1.6 gather_fusion.1
  134.1 0.1 reshape.340
  134.2 0.1 copy.90
  134.3 2.9 %fusion.6 = f32[32,2,352]{2,0,1:T(8,128)S(1)} fusion(bf16[2048,2,352]{0,2,1:T(8,128)(2,1)} %param.34, bf16[32,2048]{1,0:T(8,128)(2,1)S(1)} %fusion.39), kind=kOutput, calls=%fused_computation.10 | convolution fusion | flops 92274688 | bytes 3104768 | tf_op jit(solution)/shard_map/dot_general | solution.py:174
  137.2 1.0 convolution_convert_fusion
  138.3 13.7 %reduce-scatter.5.cloned.1.call-done = bf16[32,2,6,512]{3,0,2,1:T(8,128)(2,1)} async-done(((bf16[32,2,6,2048]{3,0,2,1:T(8,128)(2,1)}), bf16[32,2,6,512]{3,0,2,1:T(8,128)(2,1)}) %reduce-scatter.5.cloned.1.call-update) | async-done | bytes 393232 | tf_op jit(solution)/shard_map/reduce_scatter | solution.py:160
  151.9 2.1 %copy.99 = bf16[32,2,6,512]{3,1,2,0:T(2,128)(2,1)} copy(bf16[32,2,6,512]{3,0,2,1:T(8,128)(2,1)} %reduce-scatter.5.cloned.1.call-done) | data formatting | bytes 786432 | tf_op jit(solution)/shard_map/reduce_scatter | solution.py:160
  154.1 8.6 %all-to-all-start.1 = ((bf16[32,2,6,512]{3,1,2,0:T(2,128)(2,1)}), bf16[32,2,6,512]{3,1,2,0:T(2,128)(2,1)S(1)}, u32[]{:S(2)}, u32[]{:S(2)}) async-start(bf16[32,2,6,512]{3,1,2,0:T(2,128)(2,1)} %copy.99), calls=%async_computation.3 | async-start | bytes 786432 | tf_op jit(solution)/shard_map/all_to_all | solution.py:163
  162.7 0.6 multiply_divide_fusion
  163.3 0.8 copy.91
  164.0 8.8 %all-to-all-done.1 = bf16[32,2,6,512]{3,1,2,0:T(2,128)(2,1)S(1)} async-done(((bf16[32,2,6,512]{3,1,2,0:T(2,128)(2,1)}), bf16[32,2,6,512]{3,1,2,0:T(2,128)(2,1)S(1)}, u32[]{:S(2)}, u32[]{:S(2)}) %all-to-all-start.1) | async-done | bytes 393248 | tf_op jit(solution)/shard_map/all_to_all | solution.py:163
  172.8 0.9 copy.100
  173.7 1.2 reshape.318
  174.9 1.8 gather_fusion
  176.7 1.8 reshape.320
  178.4 1.3 multiply_reduce_fusion
  179.7 1.4 add_convert_fusion
  (51 shorter events, 0.6 us)
Async XLA Ops:
  6.5 14.9 %copy-start = (bf16[2048,768]{1,0:T(8,128)(2,1)S(1)}, bf16[2048,768]{1,0:T(8,128)(2,1)}, u32[]{:S(2)}) copy-start(bf16[2048,768]{1,0:T(8,128)(2,1)} %param.20) | copy-start | bytes 9437188
  6.5 69.2 %all-reduce.3.cloned.1.call-start = ((), (), s32[]{:S(2)}) async-start(), calls=%async_computation.4 | async-start | bytes 262144 | tf_op jit(solution)/shard_map/psum | solution.py:116
  21.2 2.2 %copy-start.9 = (f32[512]{0:T(512)S(1)}, f32[512]{0:T(512)}, u32[]{:S(2)}) copy-start(f32[512]{0:T(512)} %param.22) | copy-start | bytes 6148
  25.3 3.8 %copy-start.1 = (bf16[32,128,576]{1,2,0:T(8,128)(2,1)S(1)}, bf16[32,128,576]{1,2,0:T(8,128)(2,1)}, u32[]{:S(2)}) copy-start(bf16[32,128,576]{1,2,0:T(8,128)(2,1)} %param.26) | copy-start | bytes 14155780
  29.1 1.2 copy-start.6
  29.1 1.8 copy-start.3
  30.3 1.7 copy-start.11
  30.3 2.1 %copy-start.7 = (s32[32,6]{0,1:T(8,128)S(1)}, s32[32,6]{0,1:T(8,128)}, u32[]{:S(2)}) copy-start(s32[32,6]{0,1:T(8,128)} %param.31) | copy-start | bytes 2308
  30.3 45.4 %copy-start.2 = (bf16[32,2048]{1,0:T(8,128)(2,1)S(1)}, bf16[32,2048]{1,0:T(8,128)(2,1)}, u32[]{:S(2)}) copy-start(bf16[32,2048]{1,0:T(8,128)(2,1)} %param.18) | copy-start | bytes 393220
  30.3 47.1 %copy-start.8 = (f32[2048]{0:T(1024)S(1)}, f32[2048]{0:T(1024)}, u32[]{:S(2)}) copy-start(f32[2048]{0:T(1024)} %param.29) | copy-start | bytes 24580
  32.0 120.0 %reduce-scatter.5.cloned.1.call-start = ((), (), s32[]{:S(2)}) async-start(), calls=%async_computation.6 | async-start | bytes 1966080 | tf_op jit(solution)/shard_map/reduce_scatter | solution.py:160
  76.8 0.6 copy-start.5
  122.4 5.9 %copy-start.10 = (bf16[2,352,2048]{2,1,0:T(8,128)(2,1)S(1)}, bf16[2,352,2048]{2,1,0:T(8,128)(2,1)}, u32[]{:S(2)}) copy-start(bf16[2,352,2048]{2,1,0:T(8,128)(2,1)} %param.33) | copy-start | bytes 8650756
  130.4 49.3 %reduce-scatter.3.cloned.1.call-start = ((), (), s32[]{:S(2)}) async-start(), calls=%async_computation.5 | async-start | bytes 163840 | tf_op jit(solution)/shard_map/reduce_scatter | solution.py:181
  134.3 3.0 %copy-start.4 = (bf16[352,2048]{1,0:T(8,128)(2,1)S(1)}, bf16[352,2048]{1,0:T(8,128)(2,1)}, u32[]{:S(2)}) copy-start(bf16[352,2048]{1,0:T(8,128)(2,1)} %param.35) | copy-start | bytes 4325380
  154.1 18.7 %all-to-all-start.1 = ((bf16[32,2,6,512]{3,1,2,0:T(2,128)(2,1)}), bf16[32,2,6,512]{3,1,2,0:T(2,128)(2,1)S(1)}, u32[]{:S(2)}, u32[]{:S(2)}) async-start(bf16[32,2,6,512]{3,1,2,0:T(2,128)(2,1)} %copy.99), calls=%async_computation.3 | async-start | bytes 786432 | tf_op jit(solution)/shard_map/all_to_all | solution.py:163
Sparse Core Ops, SparseCore 0:
  32.1 43.5 all-reduce.2
  130.6 21.3 reduce-scatter.4
  154.4 19.3 reduce-scatter.2
where the time goes:
time: 188 us
  waiting for transfers between devices  64.4 us (34%)
  blocking collectives  42.7 us (23%)
  local copies, waits for them, and re-layouts  25.4 us (14%)
  matrix products  23.6 us (13%)
  between operations  13.4 us (7%)
  other arithmetic  9.43 us (5%)
  starting transfers between devices  8.64 us (5%)
    psum x1, waiting for transfers between devices, body(): lax.psum(partial_value.astype(jnp.bfloat16), 'head').astype(jnp.float32)  41.9 us
    all_to_all x1, blocking collectives, body(): lax.all_to_all(packed.reshape(dp_count, local_experts, capacity, ffn_inpu...  32.3 us
    reduce_scatter x1, waiting for transfers between devices, body(): lax.psum_scatter(expert_part.astype(jnp.bfloat16), 'head', scatter_dimens...  13.7 us
    all_gather x1, blocking collectives, body(): fresh_kv = lax.all_gather(fresh_part, 'head', axis=1, tiled=True)  10.4 us
    all_to_all x1, waiting for transfers between devices, body(): lax.all_to_all(expert_share, 'dp', split_axis=0, concat_axis=0, tiled=True)  8.77 us
    all_to_all x1, starting transfers between devices, body(): lax.all_to_all(expert_share, 'dp', split_axis=0, concat_axis=0, tiled=True)  8.56 us
    reshape x2, local copies, waits for them, and re-layouts, body(): packed.reshape(dp_count, local_experts, capacity, ffn_input.shape[1])  6.93 us
    dot_general x1, matrix products, body(): jnp.einsum('secd,edkf->seckf', arrived, w_experts_in, preferred_element_t...  5.86 us
  transfers between devices with their start and end apart: 4, of which 3 were waited for; matrix products, arithmetic and copies ran while one was open for 11% of the time, Pallas kernels for 0%

commit v1 on v0

--- a/solution.py
+++ b/solution.py
@@ -78,7 +78,9 @@
         "rhn,hnc->rhc", query_nope, w_key_up, preferred_element_type=jnp.float32
     ).astype(jnp.bfloat16)
     fresh_part = jnp.dot(normed, w_latent, preferred_element_type=jnp.float32).astype(jnp.bfloat16)
-    fresh_kv = lax.all_gather(fresh_part, "head", axis=1, tiled=True)
+    fresh_kv = jnp.concatenate(
+        lax.all_to_all(jnp.stack([fresh_part] * lax.axis_size("head")), "head", 0, 0), axis=1
+    )
     latent_new = rms_norm(fresh_kv[:, :LAT].astype(jnp.float32), latent_gain)
     rope_new = rotary(fresh_kv[:, LAT:].astype(jnp.float32), positions)
     key_new = jnp.concatenate([latent_new, rope_new], axis=-1).astype(jnp.bfloat16)

time: 188 us -> 187 us (level)
  blocking collectives: 42.7 us -> 32.3 us
  starting transfers between devices: 8.64 us -> 13.7 us
  local copies, waits for them, and re-layouts: 25.4 us -> 28.3 us
    all_gather x1 -> x0, blocking collectives: 10.4 us -> none  [body(): fresh_kv = lax.all_gather(fresh_part, 'head', axis=1, tiled=True)]
    all_to_all x0 -> x1, starting transfers between devices: none -> 5.01 us  [body(): lax.all_to_all(jnp.stack([fresh_part] * lax.axis_size('head')), 'head', 0...]
  transfers between devices with their start and end apart: 4 -> 5, of which waited for: 3 -> 3; matrix products, arithmetic and copies ran while one was open for 11% -> 14% of each run, Pallas kernels for 0% -> 0%
where the time goes in v1:
time: 187 us; the launch traced here: 186 us
  waiting for transfers between devices  64.7 us (35%)
  blocking collectives  32.3 us (17%)
  local copies, waits for them, and re-layouts  28.3 us (15%)
  matrix products  23.6 us (13%)
  starting transfers between devices  13.7 us (7%)
  between operations  13.4 us (7%)
  other arithmetic  9.97 us (5%)
    psum x1, waiting for transfers between devices, body(): lax.psum(partial_value.astype(jnp.bfloat16), 'head').astype(jnp.float32)  42.2 us
    all_to_all x1, blocking collectives, body(): lax.all_to_all(packed.reshape(dp_count, local_experts, capacity, ffn_inpu...  32.3 us
    reduce_scatter x1, waiting for transfers between devices, body(): lax.psum_scatter(expert_part.astype(jnp.bfloat16), 'head', scatter_dimens...  13.6 us
    all_to_all x1, waiting for transfers between devices, body(): lax.all_to_all(expert_share, 'dp', split_axis=0, concat_axis=0, tiled=True)  8.77 us
    all_to_all x1, starting transfers between devices, body(): lax.all_to_all(expert_share, 'dp', split_axis=0, concat_axis=0, tiled=True)  8.56 us
    reshape x2, local copies, waits for them, and re-layouts, body(): packed.reshape(dp_count, local_experts, capacity, ffn_input.shape[1])  6.93 us
    dot_general x1, matrix products, body(): jnp.einsum('secd,edkf->seckf', arrived, w_experts_in, preferred_element_t...  5.86 us
    scatter x1, local copies, waits for them, and re-layouts, body(): packed = jnp.zeros((slot_total, ffn_input.shape[1]), jnp.bfloat16).at[buf...  5.57 us
  transfers between devices with their start and end apart: 5, of which 3 were waited for; matrix products, arithmetic and copies ran while one was open for 14% of the time, Pallas kernels for 0%

profile of v1, /device:TPU:1, one launch (start us, length us, event | category | flops | bytes accessed | tf_op | source)
XLA Modules:
  0.0 186.0 jit_solution(16319379346289613200)
XLA Ops:
  6.5 1.2 fusion.39
  7.7 1.5 convolution_convert_fusion.4
  9.2 0.6 stack.2
  9.9 5.0 %all-to-all-start = ((bf16[4,32,144]{2,1,0:T(8,128)(2,1)}), bf16[4,32,144]{2,1,0:T(8,128)(2,1)S(1)}, u32[]{:S(2)}, u32[]{:S(2)}) async-start(bf16[4,32,144]{2,1,0:T(8,128)(2,1)} %stack.2), calls=%async_computation | async-start | bytes 131072 | tf_op jit(solution)/shard_map/all_to_all | solution.py:82
  14.9 0.7 broadcast_compare_fusion
  15.6 0.1 eq.62
  15.7 0.1 eq.57
  15.9 0.7 broadcast_multiply_fusion
  16.5 0.8 copy.109
  17.3 1.6 fusion.60
  18.9 0.1 reshape.319
  19.1 0.1 fusion.76
  19.3 0.1 copy.108
  19.4 0.1 mul.265
  19.5 0.1 eq.58
  19.6 0.6 reduce-window.6
  20.2 0.2 slice_reduce_fusion
  20.5 0.1 bitcast_bitcast_fusion
  20.6 1.2 fusion.26
  21.9 0.7 convert_element_type.107
  22.5 0.7 copy.101
  23.2 1.0 reshape.321
  24.2 0.1 fusion.49
  24.4 0.1 subtract_convert_fusion.1
  24.5 0.1 maximum_bitcast_fusion
  24.6 0.1 pad_maximum_fusion
  24.7 0.3 fusion.45
  25.0 3.4 %fusion.77 = (f32[32,4]{1,0:T(8,128)S(1)}, f32[32,4,128]{2,1,0:T(4,128)S(1)}) fusion(bf16[32,128,576]{1,2,0:T(8,128)(2,1)} %param.26, bf16[32,4,576]{2,0,1:T(8,128)(2,1)S(1)} %pad_maximum_fusion, pred[32,128]{1,0:T(8,128)(4,1)S(1)} %iota_compare_fusion.2), kind=kOutput, calls=%fused_computation.127 | convolution fusion | flops 18923392 | bytes 4936192 | tf_op jit(solution)/shard_map/rhc,rjc->rhj/dot_general | solution.py:90
  28.4 0.2 fusion.56
  28.6 0.1 copy-done.1
  28.8 1.2 fusion.23
  30.0 0.2 fusion.28
  30.3 0.3 copy-done.3
  30.6 1.1 convolution_convert_fusion.1
  31.8 42.2 %all-reduce.3.cloned.1.call-done = bf16[32,2048]{1,0:T(8,128)(2,1)} async-done(((bf16[32,2048]{1,0:T(8,128)(2,1)}), bf16[32,2048]{1,0:T(8,128)(2,1)}) %all-reduce.3.cloned.1.call-update) | async-done | bytes 131088 | tf_op jit(solution)/shard_map/psum | solution.py:118
  74.0 1.1 fusion.36
  75.0 0.6 copy-done.5
  75.7 0.1 fusion.38
  75.8 5.6 %scatter_custom_fusion = bf16[384,2048]{1,0:T(8,128)(2,1)} fusion(s32[192]{0:T(256)S(1)} %bitcast.106, bf16[32,2048]{1,0:T(8,128)(2,1)S(1)} %fusion.38, s32[1024]{0:T(1024)S(1)} %pad_clamp_fusion.1, bf16[]{:T(256)} %constant.75.clone.1), kind=kCustom, calls=%fused_computation.27 | custom fusion | bytes 1572866 | tf_op jit(solution)/shard_map/scatter | solution.py:146
  81.3 3.7 %reshape.327 = bf16[32,2,6,2048]{3,2,1,0:T(8,128)(2,1)} reshape(bf16[384,2048]{1,0:T(8,128)(2,1)} %scatter_custom_fusion) | data formatting | bytes 3145728 | tf_op jit(solution)/shard_map/reshape | solution.py:149
  85.1 3.2 %copy.112 = bf16[32,2,6,2048]{3,1,2,0:T(2,128)(2,1)S(1)} copy(bf16[32,2,6,2048]{3,2,1,0:T(8,128)(2,1)} %reshape.327) | data formatting | bytes 3145728 | tf_op jit(solution)/shard_map/reshape | solution.py:149
  88.3 32.3 %all_to_all.15 = bf16[32,2,6,2048]{3,1,2,0:T(2,128)(2,1)S(1)} all-to-all(bf16[32,2,6,2048]{3,1,2,0:T(2,128)(2,1)S(1)} %copy.112), channel_id=1, replica_groups=mesh['dp'=32,'head'=4] {'dp'}, dimensions={0} | all-to-all | bytes 3145728 | tf_op jit(solution)/shard_map/all_to_all | solution.py:148
  120.6 5.9 %fusion.15 = f32[32,2,6,2,352]{4,0,3,2,1:T(8,128)S(1)} fusion(bf16[2,2048,2,352]{1,3,2,0:T(8,128)(2,1)} %param.32, bf16[32,2,6,2048,1]{3,1,2,0,4:T(2,128)(2,1)S(1)} %bitcast.100), kind=kOutput, calls=%fused_computation.17 | convolution fusion | flops 1107296256 | bytes 8421376 | tf_op jit(solution)/shard_map/secd,edkf->seckf/dot_general | solution.py:155
  126.5 2.2 %fusion.11 = bf16[32,2,6,2048]{3,0,2,1:T(8,128)(2,1)} fusion(bf16[2,352,2048]{2,1,0:T(8,128)(2,1)S(1)} %copy-done.11, f32[32,2,6,2,352]{4,0,3,2,1:T(8,128)S(1)} %fusion.15), kind=kOutput, calls=%fused_computation.13 | convolution fusion | flops 555245568 | bytes 5537792 | tf_op jit(solution)/shard_map/secf,efd->secd/dot_general | solution.py:159
  128.8 0.1 copy.105
  128.9 0.1 reshape.347
  129.0 0.6 pad_clamp_fusion
  129.6 1.1 fusion.78
  130.7 1.6 gather_fusion.1
  132.4 0.1 reshape.350
  132.5 2.9 %fusion.6 = f32[32,2,352]{2,0,1:T(8,128)S(1)} fusion(bf16[2048,2,352]{0,2,1:T(8,128)(2,1)} %param.34, bf16[32,2048]{1,0:T(8,128)(2,1)S(1)} %fusion.38), kind=kOutput, calls=%fused_computation.10 | convolution fusion | flops 92274688 | bytes 3104768 | tf_op jit(solution)/shard_map/dot_general | solution.py:176
  135.5 1.0 convolution_convert_fusion
  136.6 13.6 %reduce-scatter.5.cloned.1.call-done = bf16[32,2,6,512]{3,0,2,1:T(8,128)(2,1)} async-done(((bf16[32,2,6,2048]{3,0,2,1:T(8,128)(2,1)}), bf16[32,2,6,512]{3,0,2,1:T(8,128)(2,1)}) %reduce-scatter.5.cloned.1.call-update) | async-done | bytes 393232 | tf_op jit(solution)/shard_map/reduce_scatter | solution.py:162
  150.2 2.1 %copy.115 = bf16[32,2,6,512]{3,1,2,0:T(2,128)(2,1)} copy(bf16[32,2,6,512]{3,0,2,1:T(8,128)(2,1)} %reduce-scatter.5.cloned.1.call-done) | data formatting | bytes 786432 | tf_op jit(solution)/shard_map/reduce_scatter | solution.py:162
  152.3 8.6 %all-to-all-start.2 = ((bf16[32,2,6,512]{3,1,2,0:T(2,128)(2,1)}), bf16[32,2,6,512]{3,1,2,0:T(2,128)(2,1)S(1)}, u32[]{:S(2)}, u32[]{:S(2)}) async-start(bf16[32,2,6,512]{3,1,2,0:T(2,128)(2,1)} %copy.115), calls=%async_computation.4 | async-start | bytes 786432 | tf_op jit(solution)/shard_map/all_to_all | solution.py:165
  160.9 0.6 multiply_divide_fusion
  161.5 0.8 copy.107
  162.3 8.8 %all-to-all-done.2 = bf16[32,2,6,512]{3,1,2,0:T(2,128)(2,1)S(1)} async-done(((bf16[32,2,6,512]{3,1,2,0:T(2,128)(2,1)}), bf16[32,2,6,512]{3,1,2,0:T(2,128)(2,1)S(1)}, u32[]{:S(2)}, u32[]{:S(2)}) %all-to-all-start.2) | async-done | bytes 393248 | tf_op jit(solution)/shard_map/all_to_all | solution.py:165
  171.1 0.9 copy.116
  172.0 1.2 reshape.328
  173.1 1.8 gather_fusion
  174.9 1.8 reshape.330
  176.7 1.3 multiply_reduce_fusion
  178.0 1.4 add_convert_fusion
  (55 shorter events, 0.8 us)
Async XLA Ops:
  6.5 10.8 %copy-start = (bf16[2048,768]{1,0:T(8,128)(2,1)S(1)}, bf16[2048,768]{1,0:T(8,128)(2,1)}, u32[]{:S(2)}) copy-start(bf16[2048,768]{1,0:T(8,128)(2,1)} %param.20) | copy-start | bytes 9437188
  9.2 10.0 %copy-start.10 = (s32[32]{0:T(128)S(1)}, s32[32]{0:T(128)}, u32[]{:S(2)}) copy-start(s32[32]{0:T(128)} %param.27) | copy-start | bytes 388
  9.9 12.7 %all-to-all-start = ((bf16[4,32,144]{2,1,0:T(8,128)(2,1)}), bf16[4,32,144]{2,1,0:T(8,128)(2,1)S(1)}, u32[]{:S(2)}, u32[]{:S(2)}) async-start(bf16[4,32,144]{2,1,0:T(8,128)(2,1)} %stack.2), calls=%async_computation | async-start | bytes 131072 | tf_op jit(solution)/shard_map/all_to_all | solution.py:82
  14.9 59.1 %all-reduce.3.cloned.1.call-start = ((), (), s32[]{:S(2)}) async-start(), calls=%async_computation.5 | async-start | bytes 262144 | tf_op jit(solution)/shard_map/psum | solution.py:118
  17.3 7.0 %copy-start.9 = (f32[512]{0:T(512)S(1)}, f32[512]{0:T(512)}, u32[]{:S(2)}) copy-start(f32[512]{0:T(512)} %param.22) | copy-start | bytes 6148
  25.0 3.8 %copy-start.1 = (bf16[32,128,576]{1,2,0:T(8,128)(2,1)S(1)}, bf16[32,128,576]{1,2,0:T(8,128)(2,1)}, u32[]{:S(2)}) copy-start(bf16[32,128,576]{1,2,0:T(8,128)(2,1)} %param.26) | copy-start | bytes 14155780
  28.8 1.2 copy-start.6
  28.8 1.8 copy-start.3
  30.0 43.9 %copy-start.2 = (bf16[32,2048]{1,0:T(8,128)(2,1)S(1)}, bf16[32,2048]{1,0:T(8,128)(2,1)}, u32[]{:S(2)}) copy-start(bf16[32,2048]{1,0:T(8,128)(2,1)} %param.18) | copy-start | bytes 393220
  30.0 45.6 %copy-start.8 = (f32[2048]{0:T(1024)S(1)}, f32[2048]{0:T(1024)}, u32[]{:S(2)}) copy-start(f32[2048]{0:T(1024)} %param.29) | copy-start | bytes 24580
  31.7 118.5 %reduce-scatter.5.cloned.1.call-start = ((), (), s32[]{:S(2)}) async-start(), calls=%async_computation.7 | async-start | bytes 1966080 | tf_op jit(solution)/shard_map/reduce_scatter | solution.py:162
  75.0 0.6 copy-start.5
  120.6 5.9 %copy-start.11 = (bf16[2,352,2048]{2,1,0:T(8,128)(2,1)S(1)}, bf16[2,352,2048]{2,1,0:T(8,128)(2,1)}, u32[]{:S(2)}) copy-start(bf16[2,352,2048]{2,1,0:T(8,128)(2,1)} %param.33) | copy-start | bytes 8650756
  126.5 2.3 %copy-start.7 = (s32[32,6]{0,1:T(8,128)S(1)}, s32[32,6]{0,1:T(8,128)}, u32[]{:S(2)}) copy-start(s32[32,6]{0,1:T(8,128)} %param.31) | copy-start | bytes 2308
  126.5 3.1 %copy-start.12 = (s32[32]{0:T(128)S(1)}, s32[32]{0:T(128)}, u32[]{:S(2)}) copy-start(s32[32]{0:T(128)} %param.28) | copy-start | bytes 388
  128.7 49.3 %reduce-scatter.3.cloned.1.call-start = ((), (), s32[]{:S(2)}) async-start(), calls=%async_computation.6 | async-start | bytes 163840 | tf_op jit(solution)/shard_map/reduce_scatter | solution.py:183
  132.5 3.0 %copy-start.4 = (bf16[352,2048]{1,0:T(8,128)(2,1)S(1)}, bf16[352,2048]{1,0:T(8,128)(2,1)}, u32[]{:S(2)}) copy-start(bf16[352,2048]{1,0:T(8,128)(2,1)} %param.35) | copy-start | bytes 4325380
  152.3 18.7 %all-to-all-start.2 = ((bf16[32,2,6,512]{3,1,2,0:T(2,128)(2,1)}), bf16[32,2,6,512]{3,1,2,0:T(2,128)(2,1)S(1)}, u32[]{:S(2)}, u32[]{:S(2)}) async-start(bf16[32,2,6,512]{3,1,2,0:T(2,128)(2,1)} %copy.115), calls=%async_computation.4 | async-start | bytes 786432 | tf_op jit(solution)/shard_map/all_to_all | solution.py:165
Sparse Core Ops, SparseCore 0:
  31.8 42.0 all-reduce.2
  128.8 21.3 reduce-scatter.4
  152.7 19.3 reduce-scatter.2
